TPU v7x, 32 devices: a whole 2x2x4 slice. The times are simulated.
32 devices in a mesh: grp: 4 (over x, core), var: 8 (over z, y).
Axes of the slice: x: 2, y: 2, z: 4, core: 2. Of those that a mesh axis runs over, the one named last changes fastest.
Arguments:
- dosages: int32 [16384, 8192], P('grp', 'var'), may hold values from 0 to 2
- variant_weight: bfloat16 [8192], P('var'), may hold values from -2 to 2
- block_id: int32 [8192], P('var'), may hold values from 0 to 127
- stack_weight: bfloat16 [1024, 64], replicated, may hold values from -0.1875 to 0.1875
- labels: int32 [16384, 64], P(('grp', 'var')), may hold values 0 or 1
Outputs:
- level_grad: float32 [1024, 64], P('var')
- weight_grad: float32 [8192], P('var')
All inputs are finite; a program needn't handle non-finite values. No bound on the sum of `labels` on one device may be relied on, other than what follows from the above.
Results may differ from a plain program's by a relative error of at most 0.00039.
Values may be sent and summed in bfloat16 or wider, within the bound.
A program may use at most 64 MiB of HBM per device.

v0:
```python
import math
import jax
import jax.numpy as jnp
from jax import lax
from jax.sharding import PartitionSpec as P


def owned_level(predictors, group_resid, norm_scale):
    owned = (
        lax.dot_general(
            predictors, group_resid, (((0,), (0,)), ((), ())), preferred_element_type=jnp.float32
        )
        * norm_scale
    )
    return lax.psum(owned, "grp")


def local(dosages, variant_weight, block_id, stack_weight, labels):
    person_rows = dosages.shape[0]
    total_preds = stack_weight.shape[0]
    var_count = lax.axis_size("var")
    per_device = total_preds // var_count
    norm_scale = 1.0 / math.sqrt(person_rows * lax.axis_size("grp"))
    dose_vals = dosages.astype(jnp.bfloat16)
    one_hot = block_id[:, None] == lax.iota(jnp.int32, per_device)[None, :]
    weighted = jnp.where(one_hot, variant_weight[:, None], jnp.zeros((), jnp.bfloat16))
    predictors = jnp.dot(dose_vals, weighted, preferred_element_type=jnp.float32).astype(
        jnp.bfloat16
    )
    regrouped = None
    regrouped = lax.all_to_all(predictors, "var", split_axis=0, concat_axis=1, tiled=True)
    logits = jnp.dot(regrouped, stack_weight, preferred_element_type=jnp.float32)
    resid = (jax.nn.sigmoid(logits) - labels.astype(jnp.float32)).astype(jnp.bfloat16)
    group_resid = None
    group_resid = lax.all_gather(resid, "var", axis=0, tiled=True)
    level_grad = owned_level(predictors, group_resid, norm_scale)
    full_grad = lax.dot_general(
        resid, stack_weight, (((1,), (1,)), ((), ())), preferred_element_type=jnp.float32
    ).astype(jnp.bfloat16)
    local_grad = lax.all_to_all(full_grad, "var", split_axis=1, concat_axis=0, tiled=True)
    column_grad = lax.dot_general(
        dose_vals, local_grad, (((0,), (0,)), ((), ())), preferred_element_type=jnp.float32
    )
    local_weight = jnp.sum(jnp.where(one_hot, column_grad, 0.0), axis=1) * norm_scale
    weight_grad = lax.psum(local_weight, "grp")
    return (level_grad, weight_grad)


def solution(mesh):
    return jax.shard_map(
        local,
        mesh=mesh,
        in_specs=(P("grp", "var"), P("var"), P("var"), P(), P(("grp", "var"), None)),
        out_specs=(P("var", None), P("var")),
        check_vma=False,
    )
```

profile of v0, /device:TPU:0, one launch (start us, length us, event | category | flops | bytes accessed | tf_op | source)
XLA Modules:
  0.0 113.5 jit_solution(6263934042086971203)
XLA Ops:
  0.6 0.0 copy-start
  0.6 0.0 copy-start.2
  0.7 8.8 %convolution_convert_fusion = bf16[128,4096]{1,0:T(8,128)(2,1)S(1)} fusion(s32[4096,1024]{1,0:T(8,128)} %param.5, s32[1024]{0:T(1024)} %param.7, bf16[1024]{0:T(1024)(128)(2,1)} %param.6), kind=kOutput, calls=%fused_computation | convolution fusion | flops 1078722560 | bytes 17831936 | tf_op jit(solution)/shard_map/dot_general | solution.py:27
  9.4 0.0 copy-start.1
  9.4 0.1 copy.14
  9.5 32.9 %all_to_all.38 = bf16[8,512,128]{1,2,0:T(8,128)(2,1)S(1)} all-to-all(bf16[8,512,128]{1,2,0:T(8,128)(2,1)S(1)} %bitcast.31), channel_id=1, replica_groups=mesh['grp'=4,'var'=8] {'var'}, dimensions={0} | all-to-all | bytes 2097152 | tf_op jit(solution)/shard_map/all_to_all | solution.py:31
  42.4 0.0 copy-done
  42.4 0.0 copy-done.2
  42.4 0.3 fusion.17
  42.8 0.4 fusion.3
  43.2 1.2 %copy.13 = bf16[64,8,8,128]{3,2,0,1:T(8,128)(2,1)} copy(bf16[64,8,8,128]{3,2,1,0:T(8,128)(2,1)S(1)} %fusion.3) | data formatting | bytes 2097152 | tf_op jit(solution)/shard_map/all_to_all | solution.py:40
  44.4 3.6 %all-to-all-start.1 = ((bf16[512,8,128]{2,0,1:T(8,128)(2,1)}), bf16[512,8,128]{2,0,1:T(8,128)(2,1)S(1)}, u32[]{:S(2)}, u32[]{:S(2)}) async-start(bf16[512,8,128]{2,0,1:T(8,128)(2,1)} %bitcast.27), calls=%async_computation.1 | async-start | bytes 2097152 | tf_op jit(solution)/shard_map/all_to_all | solution.py:40
  48.0 46.9 %all_gather.3 = bf16[4096,64]{0,1:T(8,128)(2,1)S(1)} all-gather(bf16[512,64]{0,1:T(8,128)(2,1)S(1)} %fusion.17), channel_id=1, replica_groups=mesh['grp'=4,'var'=8] {'var'}, dimensions={0}, use_global_device_ids=true | all-gather | bytes 589824 | tf_op jit(solution)/shard_map/all_gather | solution.py:35
  94.9 0.5 convolution_multiply_fusion
  95.4 0.0 all-to-all-done.1
  95.4 0.0 copy-done.1
  95.4 7.1 %fusion.10 = f32[1024]{0:T(1024)S(1)} fusion(bf16[4096,128]{1,0:T(8,128)(2,1)S(1)} %bitcast.30, s32[4096,1024]{1,0:T(8,128)} %param.5, s32[1024]{0:T(1024)S(1)} %copy-done.1), kind=kOutput, calls=%fused_computation.8 | convolution fusion | flops 1078328320 | bytes 17833984 | tf_op jit(solution)/shard_map/dot_general | solution.py:41
  102.5 11.1 %all-reduce = (f32[128,64]{0,1:T(8,128)}, f32[1024]{0:T(1024)}) all-reduce(f32[128,64]{0,1:T(8,128)S(1)} %convolution_multiply_fusion, f32[1024]{0:T(1024)S(1)} %broadcast_multiply_fusion), channel_id=1, replica_groups=mesh['grp'=4,'var'=8] {'grp'}, use_global_device_ids=true, to_apply=%region_0.1 | all-reduce | flops 9216 | bytes 73728 | tf_op jit(solution)/shard_map/psum | solution.py:15
  (1 shorter events, 0.0 us)
Async XLA Ops:
  0.6 41.8 %copy-start = (bf16[1024,64]{0,1:T(8,128)(2,1)S(1)}, bf16[1024,64]{0,1:T(8,128)(2,1)}, u32[]{:S(2)}) copy-start(bf16[1024,64]{0,1:T(8,128)(2,1)} %param.8) | copy-start | bytes 393220
  0.6 41.8 %copy-start.2 = (s32[512,64]{0,1:T(8,128)S(1)}, s32[512,64]{0,1:T(8,128)}, u32[]{:S(2)}) copy-start(s32[512,64]{0,1:T(8,128)} %param.9) | copy-start | bytes 393220
  9.4 86.0 %copy-start.1 = (s32[1024]{0:T(1024)S(1)}, s32[1024]{0:T(1024)}, u32[]{:S(2)}) copy-start(s32[1024]{0:T(1024)} %param.7) | copy-start | bytes 12292
  44.4 51.0 %all-to-all-start.1 = ((bf16[512,8,128]{2,0,1:T(8,128)(2,1)}), bf16[512,8,128]{2,0,1:T(8,128)(2,1)S(1)}, u32[]{:S(2)}, u32[]{:S(2)}) async-start(bf16[512,8,128]{2,0,1:T(8,128)(2,1)} %bitcast.27), calls=%async_computation.1 | async-start | bytes 2097152 | tf_op jit(solution)/shard_map/all_to_all | solution.py:40
where the time goes:
time: 114 us
  blocking collectives  90.8 us (80%)
  matrix products  17.1 us (15%)
  starting transfers between devices  3.6 us (3%)
  local copies, waits for them, and re-layouts  1.29 us (1%)
    all_gather x1, blocking collectives, local(): group_resid = lax.all_gather(resid, 'var', axis=0, tiled=True)  46.9 us
    all_to_all x1, blocking collectives, local(): lax.all_to_all(predictors, 'var', split_axis=0, concat_axis=1, tiled=True)  32.9 us
    psum x1, blocking collectives, owned_level(): return lax.psum(owned, 'grp')  11.1 us
    dot_general x1, matrix products, local(): jnp.dot(dose_vals, weighted, preferred_element_type=jnp.float32)  8.76 us
    dot_general x1, matrix products, local(): lax.dot_general(dose_vals, local_grad, (((0,), (0,)), ((), ())), preferre...  7.06 us
    all_to_all x1, starting transfers between devices, local(): lax.all_to_all(full_grad, 'var', split_axis=1, concat_axis=0, tiled=True)  3.6 us
  transfers between devices with their start and end apart: 1, of which 0 were waited for; matrix products, arithmetic and copies ran while one was open for 0% of the time, Pallas kernels for 0%

commit v1 on v0

--- a/solution.py
+++ b/solution.py
@@ -28,7 +28,10 @@
         jnp.bfloat16
     )
     regrouped = None
-    regrouped = lax.all_to_all(predictors, "var", split_axis=0, concat_axis=1, tiled=True)
+    regrouped = jnp.concatenate(
+        lax.all_to_all(jnp.stack(jnp.split(predictors, lax.axis_size("var"), 0), 0), "var", 0, 0),
+        axis=1,
+    )
     logits = jnp.dot(regrouped, stack_weight, preferred_element_type=jnp.float32)
     resid = (jax.nn.sigmoid(logits) - labels.astype(jnp.float32)).astype(jnp.bfloat16)
     group_resid = None

time: 114 us -> 114 us (level)
  no operation moved by 1% of the time
where the time goes in v1:
time: 114 us
  blocking collectives  90.8 us (80%)
  matrix products  17.1 us (15%)
  starting transfers between devices  3.6 us (3%)
  local copies, waits for them, and re-layouts  1.29 us (1%)
    all_gather x1, blocking collectives, local(): group_resid = lax.all_gather(resid, 'var', axis=0, tiled=True)  46.9 us
    all_to_all x1, blocking collectives, local(): lax.all_to_all(jnp.stack(jnp.split(predictors, lax.axis_size('var'), 0),...  32.9 us
    psum x1, blocking collectives, owned_level(): return lax.psum(owned, 'grp')  11.1 us
    dot_general x1, matrix products, local(): jnp.dot(dose_vals, weighted, preferred_element_type=jnp.float32)  8.76 us
    dot_general x1, matrix products, local(): lax.dot_general(dose_vals, local_grad, (((0,), (0,)), ((), ())), preferre...  7.06 us
    all_to_all x1, starting transfers between devices, local(): lax.all_to_all(full_grad, 'var', split_axis=1, concat_axis=0, tiled=True)  3.6 us
  transfers between devices with their start and end apart: 1, of which 0 were waited for; matrix products, arithmetic and copies ran while one was open for 0% of the time, Pallas kernels for 0%

profile of v1, /device:TPU:0, one launch (start us, length us, event | category | flops | bytes accessed | tf_op | source)
XLA Modules:
  0.0 113.6 jit_solution(9358059204479928694)
XLA Ops:
  0.6 0.0 copy-start
  0.6 0.0 copy-start.2
  0.7 8.8 %convolution_convert_fusion = bf16[128,4096]{1,0:T(8,128)(2,1)S(1)} fusion(s32[4096,1024]{1,0:T(8,128)} %param.5, s32[1024]{0:T(1024)} %param.7, bf16[1024]{0:T(1024)(128)(2,1)} %param.6), kind=kOutput, calls=%fused_computation | convolution fusion | flops 1078722560 | bytes 17831936 | tf_op jit(solution)/shard_map/dot_general | solution.py:27
  9.4 0.0 copy-start.1
  9.6 32.9 %all_to_all.24 = bf16[8,512,128]{1,2,0:T(8,128)(2,1)S(1)} all-to-all(bf16[8,512,128]{1,2,0:T(8,128)(2,1)S(1)} %fusion.21), channel_id=1, replica_groups=mesh['grp'=4,'var'=8] {'var'}, dimensions={0} | all-to-all | bytes 2097152 | tf_op jit(solution)/shard_map/all_to_all | solution.py:32
  42.5 0.0 copy-done
  42.5 0.0 copy-done.2
  42.5 0.3 fusion.17
  42.8 0.4 fusion.3
  43.3 1.2 %copy.10 = bf16[64,8,8,128]{3,2,0,1:T(8,128)(2,1)} copy(bf16[64,8,8,128]{3,2,1,0:T(8,128)(2,1)S(1)} %fusion.3) | data formatting | bytes 2097152 | tf_op jit(solution)/shard_map/all_to_all | solution.py:43
  44.4 3.6 %all-to-all-start.1 = ((bf16[512,8,128]{2,0,1:T(8,128)(2,1)}), bf16[512,8,128]{2,0,1:T(8,128)(2,1)S(1)}, u32[]{:S(2)}, u32[]{:S(2)}) async-start(bf16[512,8,128]{2,0,1:T(8,128)(2,1)} %bitcast.56), calls=%async_computation.1 | async-start | bytes 2097152 | tf_op jit(solution)/shard_map/all_to_all | solution.py:43
  48.0 46.9 %all_gather.3 = bf16[4096,64]{0,1:T(8,128)(2,1)S(1)} all-gather(bf16[512,64]{0,1:T(8,128)(2,1)S(1)} %fusion.17), channel_id=1, replica_groups=mesh['grp'=4,'var'=8] {'var'}, dimensions={0}, use_global_device_ids=true | all-gather | bytes 589824 | tf_op jit(solution)/shard_map/all_gather | solution.py:38
  94.9 0.5 convolution_multiply_fusion
  95.4 0.0 all-to-all-done.1
  95.4 0.0 copy-done.1
  95.4 7.1 %fusion.10 = f32[1024]{0:T(1024)S(1)} fusion(bf16[4096,128]{1,0:T(8,128)(2,1)S(1)} %bitcast.65, s32[4096,1024]{1,0:T(8,128)} %param.5, s32[1024]{0:T(1024)S(1)} %copy-done.1), kind=kOutput, calls=%fused_computation.8 | convolution fusion | flops 1078328320 | bytes 17833984 | tf_op jit(solution)/shard_map/dot_general | solution.py:44
  102.5 11.1 %all-reduce = (f32[128,64]{0,1:T(8,128)}, f32[1024]{0:T(1024)}) all-reduce(f32[128,64]{0,1:T(8,128)S(1)} %convolution_multiply_fusion, f32[1024]{0:T(1024)S(1)} %broadcast_multiply_fusion), channel_id=1, replica_groups=mesh['grp'=4,'var'=8] {'grp'}, use_global_device_ids=true, to_apply=%region_0.1 | all-reduce | flops 9216 | bytes 73728 | tf_op jit(solution)/shard_map/psum | solution.py:15
  (9 shorter events, 0.1 us)
Async XLA Ops:
  0.6 41.8 %copy-start = (bf16[1024,64]{0,1:T(8,128)(2,1)S(1)}, bf16[1024,64]{0,1:T(8,128)(2,1)}, u32[]{:S(2)}) copy-start(bf16[1024,64]{0,1:T(8,128)(2,1)} %param.8) | copy-start | bytes 393220
  0.6 41.8 %copy-start.2 = (s32[512,64]{0,1:T(8,128)S(1)}, s32[512,64]{0,1:T(8,128)}, u32[]{:S(2)}) copy-start(s32[512,64]{0,1:T(8,128)} %param.9) | copy-start | bytes 393220
  9.4 86.0 %copy-start.1 = (s32[1024]{0:T(1024)S(1)}, s32[1024]{0:T(1024)}, u32[]{:S(2)}) copy-start(s32[1024]{0:T(1024)} %param.7) | copy-start | bytes 12292
  44.4 51.0 %all-to-all-start.1 = ((bf16[512,8,128]{2,0,1:T(8,128)(2,1)}), bf16[512,8,128]{2,0,1:T(8,128)(2,1)S(1)}, u32[]{:S(2)}, u32[]{:S(2)}) async-start(bf16[512,8,128]{2,0,1:T(8,128)(2,1)} %bitcast.56), calls=%async_computation.1 | async-start | bytes 2097152 | tf_op jit(solution)/shard_map/all_to_all | solution.py:43
